TPU v7x, 32 devices: a whole 2x2x4 slice. The times are simulated.
32 devices in a mesh: dp: 2 (over core), row: 4 (over y, x), col: 4 (over z).
Axes of the slice: x: 2, y: 2, z: 4, core: 2. Of those that a mesh axis runs over, the one named last changes fastest.
Arguments:
- tokens: bfloat16 [768, 8192], P('row', ('dp', 'col')), may hold values from -6 to 6
- prefix: int32 [8], P(('dp', 'row')), may hold values from 102 to 512, as said below
- ln1_gain: float32 [768], replicated, may hold values from 0.5 to 1.5
- ln1_bias: float32 [768], replicated, may hold values from -3 to 3
- w_qkv: bfloat16 [3, 768, 768], P(None, 'row', 'col'), may hold values from -0.21875 to 0.21875
- qv_bias: float32 [2, 768], replicated, may hold values from -3 to 3
- w_out: bfloat16 [768, 768], P('col', 'row'), may hold values from -0.875 to 0.875
- out_bias: float32 [768], replicated, may hold values from -3 to 3
- ln2_gain: float32 [768], replicated, may hold values from 0.5 to 1.5
- ln2_bias: float32 [768], replicated, may hold values from -3 to 3
- w_fc: bfloat16 [768, 3072], P('row', 'col'), may hold values from -0.21875 to 0.21875
- fc_bias: float32 [3072], replicated, may hold values from -3 to 3
- w_proj: bfloat16 [768, 3072], P('row', 'col'), may hold values from -0.109375 to 0.109375
- proj_bias: float32 [768], replicated, may hold values from -3 to 3
- cotangent: bfloat16 [768, 8192], P('row', ('dp', 'col')), may hold values from -6 to 6
Outputs:
- output: bfloat16 [768, 8192], P('row', ('dp', 'col'))
- input_grad: float32 [768, 8192], P('row', ('dp', 'col'))
- ln1_gain_grad: float32 [768], replicated
- ln1_bias_grad: float32 [768], replicated
- w_qkv_grad: float32 [3, 768, 768], P(None, 'row', 'col')
- qv_bias_grad: float32 [2, 768], replicated
- w_out_grad: float32 [768, 768], P('col', 'row')
- out_bias_grad: float32 [768], replicated
- ln2_gain_grad: float32 [768], replicated
- ln2_bias_grad: float32 [768], replicated
- w_fc_grad: float32 [768, 3072], P('row', 'col')
- fc_bias_grad: float32 [3072], replicated
- w_proj_grad: float32 [768, 3072], P('row', 'col')
- proj_bias_grad: float32 [768], replicated
Inputs may be any that keep to these rules, and one draw needn't show every extreme that they name: `prefix`: in every draw some sequence has exactly 102 and some other exactly 512.
All inputs are finite; a program needn't handle non-finite values.
Results may differ from a plain program's by a relative error of at most 0.012.
Values may be sent and summed in bfloat16 or wider, within the bound.
A program may use at most 256 MiB of HBM per device.

v0:
```python
import jax
import jax.numpy as jnp
from jax import lax
from jax.sharding import PartitionSpec as P

D = 768
FF = 3072
HEAD_DIM = 64
LEN = 1024
epsilon = 1e-05
masked_score = -1e30


def feature_totals(values):
    return lax.psum(values, "row")


def column_rows(values):
    return lax.all_gather(values, "col", axis=0, tiled=True)


def row_rows(values):
    return lax.all_gather(values, "row", axis=0, tiled=True)


def summed_over_row(term_fn, row_count):
    return lax.psum_scatter(
        term_fn(jnp.int32(0), row_count * lax.axis_size("row")),
        "row",
        scatter_dimension=0,
        tiled=True,
    )


def summed_over_col(term_fn, row_count):
    return lax.psum_scatter(
        term_fn(jnp.int32(0), row_count * lax.axis_size("col")),
        "col",
        scatter_dimension=0,
        tiled=True,
    )


def take_portion(complete, position, portion_size, along):
    return lax.dynamic_slice_in_dim(complete, position * portion_size, portion_size, along)


def place_portion(portion, position, full_size, along):
    zeroed_shape = portion.shape[:along] + (full_size,) + portion.shape[along + 1 :]
    zeroed = jnp.zeros(zeroed_shape, jnp.float32)
    return lax.dynamic_update_slice_in_dim(zeroed, portion, position * portion.shape[along], along)


def gelu_tanh(values):
    return jax.nn.gelu(values, approximate=True)


def norm_forward(values, norm_gain, norm_offset, totals_fn):
    plain_sum, square_sum = totals_fn((jnp.sum(values, axis=1), jnp.sum(values * values, axis=1)))
    center = (plain_sum / D)[:, None]
    inverse = lax.rsqrt(square_sum[:, None] / D - center * center + epsilon)
    unit_rows = (values - center) * inverse
    return (unit_rows * norm_gain + norm_offset, unit_rows, inverse)


def norm_backward(grad_rows, unit_rows, inverse, norm_gain, totals_fn):
    scaled = grad_rows * norm_gain
    plain_sum, cross_sum = totals_fn((jnp.sum(scaled, axis=1), jnp.sum(scaled * unit_rows, axis=1)))
    return inverse * (scaled - (plain_sum / D)[:, None] - unit_rows * (cross_sum / D)[:, None])


def split_heads(flat_rows):
    return flat_rows.reshape(LEN, flat_rows.shape[1] // HEAD_DIM, HEAD_DIM)


def scores_of(queries, keys_block, limit_value):
    raw_scores = jnp.einsum("qhe,khe->hqk", queries, keys_block, preferred_element_type=jnp.float32)
    raw_scores = raw_scores * HEAD_DIM ** (-0.5)
    places = jnp.arange(LEN, dtype=jnp.int32)
    visible = (places[None, :] <= places[:, None]) | (places[None, :] < limit_value)
    return jnp.where(visible[None], raw_scores, masked_score)


def attend_forward(packed):
    block_rows, limit_value = packed
    queries = split_heads(block_rows[:, 0])
    keys_block = split_heads(block_rows[:, 1])
    values_block = split_heads(block_rows[:, 2])
    scores = scores_of(queries, keys_block, limit_value)
    largest = jnp.max(scores, axis=-1, keepdims=True)
    weights = jnp.exp(scores - largest)
    row_totals = jnp.sum(weights, axis=-1, keepdims=True)
    probs = (weights / row_totals).astype(jnp.bfloat16)
    mixed = jnp.einsum("hqk,khe->qhe", probs, values_block, preferred_element_type=jnp.float32)
    return (mixed.reshape(LEN, -1).astype(jnp.bfloat16), (largest + jnp.log(row_totals))[..., 0])


def attend_backward(packed):
    block_rows, limit_value, log_total, out_grad = packed
    queries = split_heads(block_rows[:, 0])
    keys_block = split_heads(block_rows[:, 1])
    values_block = split_heads(block_rows[:, 2])
    scores = scores_of(queries, keys_block, limit_value)
    probs = jnp.exp(scores - log_total[..., None])
    probs_low = probs.astype(jnp.bfloat16)
    grad_heads = split_heads(out_grad)
    weight_grad = jnp.einsum(
        "qhe,khe->hqk", grad_heads, values_block, preferred_element_type=jnp.float32
    )
    row_inner = jnp.sum(probs * weight_grad, axis=-1, keepdims=True)
    score_grad = (probs * (weight_grad - row_inner)).astype(jnp.bfloat16)
    query_grad = jnp.einsum(
        "hqk,khe->qhe", score_grad, keys_block, preferred_element_type=jnp.float32
    )
    key_grad = jnp.einsum("hqk,qhe->khe", score_grad, queries, preferred_element_type=jnp.float32)
    value_grad = jnp.einsum(
        "hqk,qhe->khe", probs_low, grad_heads, preferred_element_type=jnp.float32
    )
    score_factor = HEAD_DIM ** (-0.5)
    stacked = jnp.stack(
        [
            (query_grad * score_factor).reshape(LEN, -1),
            (key_grad * score_factor).reshape(LEN, -1),
            value_grad.reshape(LEN, -1),
        ],
        axis=1,
    )
    return stacked.astype(jnp.bfloat16)


def on_device(
    tokens,
    prefix,
    ln1_gain,
    ln1_bias,
    w_qkv,
    qv_bias,
    w_out,
    out_bias,
    ln2_gain,
    ln2_bias,
    w_fc,
    fc_bias,
    w_proj,
    proj_bias,
    cotangent,
):
    row_place = lax.axis_index("row")
    col_place = lax.axis_index("col")
    row_devices = lax.axis_size("row")
    col_devices = lax.axis_size("col")
    width_row, local_rows = tokens.shape
    width_col = w_qkv.shape[2]
    hidden_col = w_fc.shape[1]
    seq_rows = local_rows * col_devices // row_devices
    seq_count = seq_rows // LEN
    residual = tokens.T.astype(jnp.float32)
    cotangent_local = cotangent.T
    first_gain = take_portion(ln1_gain, row_place, width_row, 0)
    first_normed, first_unit, first_inverse = norm_forward(
        residual, first_gain, take_portion(ln1_bias, row_place, width_row, 0), feature_totals
    )
    first_gathered = column_rows(first_normed.astype(jnp.bfloat16))

    def qkv_term(first_row, row_count):
        return jnp.einsum("td,sde->tse", first_gathered, w_qkv, preferred_element_type=jnp.float32)

    bias_col = take_portion(qv_bias, col_place, width_col, 1)
    bias_rows = jnp.stack([bias_col[0], jnp.zeros_like(bias_col[0]), bias_col[1]])
    qkv_sum = summed_over_row(qkv_term, seq_rows)
    qkv = (qkv_sum + bias_rows).astype(jnp.bfloat16)
    blocks = qkv.reshape(seq_count, LEN, 3, width_col)
    attn_blocks, log_totals = lax.map(attend_forward, (blocks, prefix))
    attn = attn_blocks.reshape(seq_rows, width_col)
    attn_gathered = row_rows(attn)

    def out_term(first_row, row_count):
        return jnp.dot(attn_gathered, w_out, preferred_element_type=jnp.float32)

    middle = (
        residual
        + summed_over_col(out_term, local_rows)
        + take_portion(out_bias, row_place, width_row, 0)
    )
    grad_output = cotangent_local.astype(jnp.float32)
    second_gain = take_portion(ln2_gain, row_place, width_row, 0)
    second_normed, second_unit, second_inverse = norm_forward(
        middle, second_gain, take_portion(ln2_bias, row_place, width_row, 0), feature_totals
    )
    second_gathered = column_rows(second_normed.astype(jnp.bfloat16))

    def up_term(first_row, row_count):
        return jnp.dot(second_gathered, w_fc, preferred_element_type=jnp.float32)

    hidden = summed_over_row(up_term, seq_rows) + take_portion(fc_bias, col_place, hidden_col, 0)
    active, gelu_pull = jax.vjp(gelu_tanh, hidden)
    active_gathered = row_rows(active.astype(jnp.bfloat16))

    def down_term(first_row, row_count):
        return jnp.einsum("tf,df->td", active_gathered, w_proj, preferred_element_type=jnp.float32)

    final_rows = (
        middle
        + summed_over_col(down_term, local_rows)
        + take_portion(proj_bias, row_place, width_row, 0)
    )
    output = final_rows.astype(jnp.bfloat16)
    grad_gathered = column_rows(cotangent_local)
    w_proj_grad = jnp.einsum(
        "tf,td->df", active_gathered, grad_gathered, preferred_element_type=jnp.float32
    )

    def active_term(first_row, row_count):
        return jnp.einsum("td,df->tf", grad_gathered, w_proj, preferred_element_type=jnp.float32)

    hidden_grad = gelu_pull(summed_over_row(active_term, seq_rows))[0].astype(jnp.bfloat16)
    hidden_gathered = row_rows(hidden_grad)
    w_fc_grad = jnp.einsum(
        "td,tf->df", second_gathered, hidden_gathered, preferred_element_type=jnp.float32
    )

    def second_term(first_row, row_count):
        return jnp.einsum("tf,df->td", hidden_gathered, w_fc, preferred_element_type=jnp.float32)

    second_grad = summed_over_col(second_term, local_rows)
    middle_grad = grad_output + norm_backward(
        second_grad, second_unit, second_inverse, second_gain, feature_totals
    )
    ln2_gain_part = place_portion(jnp.sum(second_grad * second_unit, axis=0), row_place, D, 0)
    ln2_bias_part = place_portion(jnp.sum(second_grad, axis=0), row_place, D, 0)
    fc_bias_part = place_portion(jnp.sum(hidden_grad.astype(jnp.float32), axis=0), col_place, FF, 0)
    proj_bias_part = place_portion(jnp.sum(grad_output, axis=0), row_place, D, 0)
    branch_grad = middle_grad.astype(jnp.bfloat16)
    branch_gathered = column_rows(branch_grad)
    w_out_grad = jnp.einsum(
        "te,td->ed", attn_gathered, branch_gathered, preferred_element_type=jnp.float32
    )

    def attn_term(first_row, row_count):
        return jnp.einsum("td,ed->te", branch_gathered, w_out, preferred_element_type=jnp.float32)

    attn_grad = summed_over_row(attn_term, seq_rows).astype(jnp.bfloat16)
    qkv_grad = lax.map(
        attend_backward, (blocks, prefix, log_totals, attn_grad.reshape(seq_count, LEN, width_col))
    )
    qkv_grad = qkv_grad.reshape(seq_rows, 3, width_col)
    qkv_gathered = row_rows(qkv_grad)
    w_qkv_grad = jnp.einsum(
        "td,tse->sde", first_gathered, qkv_gathered, preferred_element_type=jnp.float32
    )

    def first_term(first_row, row_count):
        return jnp.einsum("tse,sde->td", qkv_gathered, w_qkv, preferred_element_type=jnp.float32)

    first_grad = summed_over_col(first_term, local_rows)
    input_grad = middle_grad + norm_backward(
        first_grad, first_unit, first_inverse, first_gain, feature_totals
    )
    qkv_totals = jnp.sum(qkv_grad.astype(jnp.float32), axis=0)
    qv_part = place_portion(jnp.stack([qkv_totals[0], qkv_totals[2]]), col_place, D, 1)
    out_bias_part = place_portion(jnp.sum(branch_grad.astype(jnp.float32), axis=0), row_place, D, 0)
    ln1_gain_part = place_portion(jnp.sum(first_grad * first_unit, axis=0), row_place, D, 0)
    ln1_bias_part = place_portion(jnp.sum(first_grad, axis=0), row_place, D, 0)
    vectors = lax.psum(
        (
            ln1_gain_part,
            ln1_bias_part,
            qv_part,
            out_bias_part,
            ln2_gain_part,
            ln2_bias_part,
            fc_bias_part,
            proj_bias_part,
        ),
        ("dp", "row", "col"),
    )
    matrices = (
        lax.psum(w_qkv_grad.astype(jnp.bfloat16), "dp").astype(jnp.float32),
        lax.psum(w_out_grad.astype(jnp.bfloat16), "dp").astype(jnp.float32),
        lax.psum(w_fc_grad.astype(jnp.bfloat16), "dp").astype(jnp.float32),
        lax.psum(w_proj_grad.astype(jnp.bfloat16), "dp").astype(jnp.float32),
    )
    return (
        output.T,
        input_grad.T,
        vectors[0],
        vectors[1],
        matrices[0],
        vectors[2],
        matrices[1],
        vectors[3],
        vectors[4],
        vectors[5],
        matrices[2],
        vectors[6],
        matrices[3],
        vectors[7],
    )


def solution(mesh):
    placed = (
        P("row", ("dp", "col")),
        P(("dp", "row")),
        P(),
        P(),
        P(None, "row", "col"),
        P(),
        P("col", "row"),
        P(),
        P(),
        P(),
        P("row", "col"),
        P(),
        P("row", "col"),
        P(),
        P("row", ("dp", "col")),
    )
    return jax.shard_map(
        on_device,
        mesh=mesh,
        in_specs=placed,
        out_specs=(
            P("row", ("dp", "col")),
            P("row", ("dp", "col")),
            P(),
            P(),
            P(None, "row", "col"),
            P(),
            P("col", "row"),
            P(),
            P(),
            P(),
            P("row", "col"),
            P(),
            P("row", "col"),
            P(),
        ),
        check_vma=False,
    )
```

profile of v0, /device:TPU:0, one launch (start us, length us, event | category | flops | bytes accessed | tf_op | source)
XLA Modules:
  0.0 1165.3 jit_solution(17599242956197801233)
XLA Ops:
  7.2 1.1 convert_reduce_fusion.3
  8.3 1.1 fusion.45
  11.0 11.5 all-reduce.4
  22.5 1.9 fusion.38
  24.5 1.1 copy.29
  25.6 35.4 %all-gather.9.cloned.1.call-done = bf16[4096,192]{0,1:T(8,128)(2,1)} async-done(((bf16[1024,192]{0,1:T(8,128)(2,1)}), bf16[4096,192]{0,1:T(8,128)(2,1)}) %all-gather.9.cloned.1.call-update) | async-done | bytes 1572880 | tf_op jit(solution)/shard_map/all_gather | solution.py:19
  61.1 6.4 fusion.61
  69.5 92.0 %reduce-scatter.9.cloned.1.call-done = f32[1024,3,192]{0,2,1:T(8,128)} async-done(((f32[4096,3,192]{0,2,1:T(8,128)}), f32[1024,3,192]{0,2,1:T(8,128)}) %reduce-scatter.9.cloned.1.call-update) | async-done | bytes 2359312 | tf_op jit(solution)/shard_map/reduce_scatter | solution.py:27
  161.5 1.9 add_convert_fusion
  163.5 3.2 fusion.55
  166.8 1.7 fusion
  168.5 2.8 copy-done.2
  171.3 3.0 fusion.21
  174.4 31.1 %all-gather.11.cloned.1.call-done = bf16[4096,192]{0,1:T(8,128)(2,1)} async-done(((bf16[1024,192]{0,1:T(8,128)(2,1)}), bf16[4096,192]{0,1:T(8,128)(2,1)}) %all-gather.11.cloned.1.call-update) | async-done | bytes 1572880 | tf_op jit(solution)/shard_map/all_gather | solution.py:23
  205.5 3.7 fusion.56
  212.1 57.5 %reduce-scatter.11.cloned.1.call-done = f32[1024,192]{0,1:T(8,128)} async-done(((f32[4096,192]{0,1:T(8,128)}), f32[1024,192]{0,1:T(8,128)}) %reduce-scatter.11.cloned.1.call-update) | async-done | bytes 786448 | tf_op jit(solution)/shard_map/reduce_scatter | solution.py:36
  269.6 1.3 fusion.49
  270.9 10.1 all-reduce.3
  281.0 1.0 add_convert_fusion.2
  282.1 26.1 %all-gather.17.cloned.1.call-done = bf16[4096,192]{0,1:T(8,128)(2,1)} async-done(((bf16[1024,192]{0,1:T(8,128)(2,1)}), bf16[4096,192]{0,1:T(8,128)(2,1)}) %all-gather.17.cloned.1.call-update) | async-done | bytes 1572880 | tf_op jit(solution)/shard_map/all_gather | solution.py:19
  308.2 7.7 fusion.59
  316.2 30.0 %all-gather.13.cloned.1.call-done = bf16[4096,192]{0,1:T(8,128)(2,1)} async-done(((bf16[1024,192]{0,1:T(8,128)(2,1)}), bf16[4096,192]{0,1:T(8,128)(2,1)}) %all-gather.13.cloned.1.call-update) | async-done | bytes 1572880 | tf_op jit(solution)/shard_map/all_gather | solution.py:19
  346.2 7.9 fusion.57
  354.9 114.0 %reduce-scatter.17.cloned.1.call-done = f32[1024,768]{1,0:T(8,128)} async-done(((f32[4096,768]{1,0:T(8,128)}), f32[1024,768]{1,0:T(8,128)}) %reduce-scatter.17.cloned.1.call-update) | async-done | bytes 3145744 | tf_op jit(solution)/shard_map/reduce_scatter | solution.py:27
  468.9 123.9 %reduce-scatter.13.cloned.1.call-done = f32[1024,768]{1,0:T(8,128)} async-done(((f32[4096,768]{1,0:T(8,128)}), f32[1024,768]{1,0:T(8,128)}) %reduce-scatter.13.cloned.1.call-update) | async-done | bytes 3145744 | tf_op jit(solution)/shard_map/reduce_scatter | solution.py:27
  592.7 5.6 convert_reduce_fusion
  598.5 70.2 %all-gather.19.cloned.1.call-done = bf16[4096,768]{1,0:T(8,128)(2,1)} async-done(((bf16[1024,768]{1,0:T(8,128)(2,1)}), bf16[4096,768]{1,0:T(8,128)(2,1)}) %all-gather.19.cloned.1.call-update) | async-done | bytes 6291472 | tf_op jit(solution)/shard_map/all_gather | solution.py:23
  668.7 6.6 fusion.60
  675.4 60.4 %reduce-scatter.19.cloned.1.call-done = f32[1024,192]{0,1:T(8,128)} async-done(((f32[4096,192]{0,1:T(8,128)}), f32[1024,192]{0,1:T(8,128)}) %reduce-scatter.19.cloned.1.call-update) | async-done | bytes 786448 | tf_op jit(solution)/shard_map/reduce_scatter | solution.py:36
  735.8 1.5 multiply_reduce_fusion.1
  737.3 10.1 all-reduce.2
  747.3 2.2 convert_reduce_fusion.4
  749.7 35.4 %all-gather.21.cloned.1.call-done = bf16[4096,192]{0,1:T(8,128)(2,1)} async-done(((bf16[1024,192]{0,1:T(8,128)(2,1)}), bf16[4096,192]{0,1:T(8,128)(2,1)}) %all-gather.21.cloned.1.call-update) | async-done | bytes 1572880 | tf_op jit(solution)/shard_map/all_gather | solution.py:19
  785.0 3.7 fusion.62
  789.8 41.9 %reduce-scatter.21.cloned.1.call-done = f32[1024,192]{0,1:T(8,128)} async-done(((f32[4096,192]{0,1:T(8,128)}), f32[1024,192]{0,1:T(8,128)}) %reduce-scatter.21.cloned.1.call-update) | async-done | bytes 786448 | tf_op jit(solution)/shard_map/reduce_scatter | solution.py:27
  831.7 1.2 convert_element_type.111
  833.0 6.1 multiply_reduce_fusion
  839.1 0.9 slice-done.1
  840.0 1.8 slice-done.2
  841.8 5.2 multiply_convert_fusion
  847.0 4.2 fusion.16
  851.6 2.0 fusion.17
  853.7 2.1 fusion.18
  855.7 1.3 convert_reduce_fusion.1
  857.6 4.9 convolution_convert_fusion.1
  862.4 41.3 %all-gather.15.cloned.1.call-done = bf16[4096,768]{1,0:T(8,128)(2,1)} async-done(((bf16[1024,768]{1,0:T(8,128)(2,1)}), bf16[4096,768]{1,0:T(8,128)(2,1)}) %all-gather.15.cloned.1.call-update) | async-done | bytes 6291472 | tf_op jit(solution)/shard_map/all_gather | solution.py:23
  903.8 5.5 fusion.25
  909.2 1.2 convolution_convert_fusion.2
  910.5 52.1 %all-gather.23.cloned.1.call-done = bf16[4096,3,192]{0,2,1:T(8,128)(2,1)} async-done(((bf16[1024,3,192]{0,2,1:T(8,128)(2,1)}), bf16[4096,3,192]{0,2,1:T(8,128)(2,1)}) %all-gather.23.cloned.1.call-update) | async-done | bytes 4718608 | tf_op jit(solution)/shard_map/all_gather | solution.py:23
  962.6 5.0 fusion.26
  967.9 5.4 convolution_bitcast_fusion
  973.4 0.9 copy-done.16
  974.3 6.8 fusion.58
  983.0 4.3 all-reduce.8.cloned.1.call-done
  987.3 1.8 convert_element_type.122
  989.1 1.8 convert_element_type.126
  990.9 1.9 copy.34
  992.8 1.6 convert_element_type.119
  994.5 56.6 %reduce-scatter.23.cloned.1.call-done = f32[1024,192]{0,1:T(8,128)} async-done(((f32[4096,192]{0,1:T(8,128)}), f32[1024,192]{0,1:T(8,128)}) %reduce-scatter.23.cloned.1.call-update) | async-done | bytes 786448 | tf_op jit(solution)/shard_map/reduce_scatter | solution.py:36
  1051.0 1.5 fusion.44
  1052.5 10.1 all-reduce.1
  1062.7 51.0 %reduce-scatter.15.cloned.1.call-done = f32[1024,192]{0,1:T(8,128)} async-done(((f32[4096,192]{0,1:T(8,128)}), f32[1024,192]{0,1:T(8,128)}) %reduce-scatter.15.cloned.1.call-update) | async-done | bytes 786448 | tf_op jit(solution)/shard_map/reduce_scatter | solution.py:36
  1113.6 2.9 fusion.43
  1117.1 41.7 %all-reduce = (f32[768]{0:T(1024)}, f32[768]{0:T(1024)}, f32[2,768]{1,0:T(2,128)}, f32[768]{0:T(1024)}, f32[768]{0:T(1024)}, /*index=5*/f32[768]{0:T(1024)}, f32[3072]{0:T(1024)}, f32[768]{0:T(1024)}) all-reduce(f32[768]{0:T(1024)S(1)} %dynamic_update_slice.33, ...), channel_id=1, replica_groups=mesh['dp'=2,'row'=4,'col'=4] {'dp','row','col'}, use_global_device_ids=true, to_apply=%region_28.29 | all-reduce | flops 9216 | bytes 73728 | tf_op jit(solution)/shard_map/psum | solution.py:264
  (110 shorter events, 12.4 us)
Async XLA Ops:
  7.2 339.0 %copy-start = (bf16[192,768]{1,0:T(8,128)(2,1)S(1)}, bf16[192,768]{1,0:T(8,128)(2,1)}, u32[]{:S(2)}) copy-start(bf16[192,768]{1,0:T(8,128)(2,1)} %param.25) | copy-start | bytes 884740
  7.2 53.9 %all-gather.9.cloned.1.call-start = ((), (), s32[]{:S(2)}) async-start(), calls=%async_computation.8 | async-start | bytes 1966080 | tf_op jit(solution)/shard_map/all_gather | solution.py:19
  24.4 137.1 %reduce-scatter.9.cloned.1.call-start = ((), (), s32[]{:S(2)}) async-start(), calls=%async_computation.9 | async-start | bytes 11796480 | tf_op jit(solution)/shard_map/reduce_scatter | solution.py:27
  67.5 137.9 %all-gather.11.cloned.1.call-start = ((), (), s32[]{:S(2)}) async-start(), calls=%async_computation.10 | async-start | bytes 1966080 | tf_op jit(solution)/shard_map/all_gather | solution.py:23
  163.5 3.3 copy-start.8
  163.5 5.0 copy-start.11
  166.7 4.6 copy-start.2
  171.3 34.1 %copy-start.17 = (bf16[192,192]{1,0:T(8,128)(2,1)S(1)}, bf16[192,192]{1,0:T(8,128)(2,1)}, u32[]{:S(2)}) copy-start(bf16[192,192]{1,0:T(8,128)(2,1)} %param.21) | copy-start | bytes 221188
  174.3 95.3 %reduce-scatter.11.cloned.1.call-start = ((), (), s32[]{:S(2)}) async-start(), calls=%async_computation.11 | async-start | bytes 3932160 | tf_op jit(solution)/shard_map/reduce_scatter | solution.py:36
  209.2 60.4 %copy-start.4 = (bf16[192,1024]{1,0:T(8,128)(2,1)S(1)}, bf16[192,1024]{1,0:T(8,128)(2,1)}, u32[]{:S(2)}) copy-start(bf16[192,1024]{1,0:T(8,128)(2,1)} %param.15) | copy-start | bytes 1179652
  209.2 99.0 %copy-start.15 = (bf16[192,768]{1,0:T(8,128)(2,1)S(1)}, bf16[192,768]{1,0:T(8,128)(2,1)}, u32[]{:S(2)}) copy-start(bf16[192,768]{1,0:T(8,128)(2,1)} %param.27) | copy-start | bytes 884740
  209.2 99.0 %all-gather.17.cloned.1.call-start = ((), (), s32[]{:S(2)}) async-start(), calls=%async_computation.16 | async-start | bytes 1966080 | tf_op jit(solution)/shard_map/all_gather | solution.py:19
  209.8 136.4 %all-gather.13.cloned.1.call-start = ((), (), s32[]{:S(2)}) async-start(), calls=%async_computation.12 | async-start | bytes 1966080 | tf_op jit(solution)/shard_map/all_gather | solution.py:19
  282.0 186.9 %reduce-scatter.17.cloned.1.call-start = ((), (), s32[]{:S(2)}) async-start(), calls=%async_computation.17 | async-start | bytes 15728640 | tf_op jit(solution)/shard_map/reduce_scatter | solution.py:27
  315.9 276.8 %reduce-scatter.13.cloned.1.call-start = ((), (), s32[]{:S(2)}) async-start(), calls=%async_computation.13 | async-start | bytes 15728640 | tf_op jit(solution)/shard_map/reduce_scatter | solution.py:27
  354.0 314.7 %all-gather.19.cloned.1.call-start = ((), (), s32[]{:S(2)}) async-start(), calls=%async_computation.18 | async-start | bytes 7864320 | tf_op jit(solution)/shard_map/all_gather | solution.py:23
  598.4 137.4 %reduce-scatter.19.cloned.1.call-start = ((), (), s32[]{:S(2)}) async-start(), calls=%async_computation.19 | async-start | bytes 3932160 | tf_op jit(solution)/shard_map/reduce_scatter | solution.py:36
  675.3 72.0 %copy-start.7 = (bf16[192,1024]{1,0:T(8,128)(2,1)S(1)}, bf16[192,1024]{1,0:T(8,128)(2,1)}, u32[]{:S(2)}) copy-start(bf16[192,1024]{1,0:T(8,128)(2,1)} %param.29) | copy-start | bytes 1179652
  675.4 109.6 %all-gather.21.cloned.1.call-start = ((), (), s32[]{:S(2)}) async-start(), calls=%async_computation.20 | async-start | bytes 1966080 | tf_op jit(solution)/shard_map/all_gather | solution.py:19
  749.6 82.1 %reduce-scatter.21.cloned.1.call-start = ((), (), s32[]{:S(2)}) async-start(), calls=%async_computation.21 | async-start | bytes 3932160 | tf_op jit(solution)/shard_map/reduce_scatter | solution.py:27
  788.7 44.2 %copy-start.12 = (bf16[1024,1,192]{0,2,1:T(8,128)(2,1)S(1)}, bf16[1024,1,192]{0,2,1:T(8,128)(2,1)}, u32[]{:S(2)}) copy-start(bf16[1024,1,192]{0,2,1:T(8,128)(2,1)} %copy-done.11) | copy-start | bytes 1179652
  788.8 115.0 %all-gather.15.cloned.1.call-start = ((), (), s32[]{:S(2)}) async-start(), calls=%async_computation.14 | async-start | bytes 7864320 | tf_op jit(solution)/shard_map/all_gather | solution.py:23
  789.5 173.0 %all-gather.23.cloned.1.call-start = ((), (), s32[]{:S(2)}) async-start(), calls=%async_computation.22 | async-start | bytes 5898240 | tf_op jit(solution)/shard_map/all_gather | solution.py:23
  832.9 6.2 slice-start
  832.9 7.1 slice-start.1
  833.0 8.8 slice-start.2
  841.8 5.2 copy-start.9
  847.0 4.6 copy-start.3
  855.7 1.8 copy-start.10
  857.0 130.3 %all-reduce.8.cloned.1.call-start = ((), (), s32[]{:S(2)}) async-start(), calls=%async_computation.24 | async-start | bytes 1966080 | tf_op jit(solution)/shard_map/psum | solution.py:278
  862.4 46.8 %copy-start.6 = (bf16[4096,192]{0,1:T(8,128)(2,1)S(1)}, bf16[4096,192]{0,1:T(8,128)(2,1)}, u32[]{:S(2)}) copy-start(bf16[4096,192]{0,1:T(8,128)(2,1)} %all-gather.11.cloned.1.call-done) | copy-start | bytes 4718596
  903.8 5.5 copy-start.13
  910.5 57.4 %copy-start.14 = (bf16[3,192,192]{2,1,0:T(8,128)(2,1)S(1)}, bf16[3,192,192]{2,1,0:T(8,128)(2,1)}, u32[]{:S(2)}) copy-start(bf16[3,192,192]{2,1,0:T(8,128)(2,1)} %param.19) | copy-start | bytes 663556
  967.5 83.5 %reduce-scatter.23.cloned.1.call-start = ((), (), s32[]{:S(2)}) async-start(), calls=%async_computation.23 | async-start | bytes 3932160 | tf_op jit(solution)/shard_map/reduce_scatter | solution.py:36
  973.3 1.0 copy-start.16
  973.3 140.3 %reduce-scatter.15.cloned.1.call-start = ((), (), s32[]{:S(2)}) async-start(), calls=%async_computation.15 | async-start | bytes 3932160 | tf_op jit(solution)/shard_map/reduce_scatter | solution.py:36
  981.1 132.5 %copy-start.5 = (f32[1024,192]{0,1:T(8,128)S(1)}, f32[1024,192]{0,1:T(8,128)}, u32[]{:S(2)}) copy-start(f32[1024,192]{0,1:T(8,128)} %reduce-scatter.19.cloned.1.call-done) | copy-start | bytes 2359300
  992.8 165.9 %copy-start.1 = (bf16[192,768]{1,0:T(8,128)(2,1)S(1)}, bf16[192,768]{1,0:T(8,128)(2,1)}, u32[]{:S(2)}) copy-start(bf16[192,768]{1,0:T(8,128)(2,1)} %param.25) | copy-start | bytes 884740
Sparse Core Ops, SparseCore 0:
  24.6 36.4 all-gather.8
  67.6 93.8 reduce-scatter.8
  174.4 30.9 all-gather.10
  209.3 60.2 reduce-scatter.10
  271.0 37.1 all-gather.16
  310.2 35.9 all-gather.12
  349.3 119.5 reduce-scatter.16
  472.0 120.7 reduce-scatter.12
  598.5 70.1 all-gather.18
  675.5 60.2 reduce-scatter.18
  749.7 35.2 all-gather.20
  788.9 42.8 reduce-scatter.20
  833.6 70.1 all-gather.14
  905.5 57.0 all-gather.22
  967.7 19.5 all-reduce.7
  989.5 61.4 reduce-scatter.22
  1053.3 60.2 reduce-scatter.14
where the time goes:
time: 1170 us
  waiting for transfers between devices  924 us (79%)
  matrix products  85.4 us (7%)
  blocking collectives  83.4 us (7%)
  other arithmetic  37.2 us (3%)
  local copies, waits for them, and re-layouts  18.6 us (2%)
  between operations  15 us (1%)
    reduce_scatter x4, waiting for transfers between devices, summed_over_row(): lax.psum_scatter(term_fn(jnp.int32(0), row_count * lax.axis_size('row')),...  372 us
    reduce_scatter x4, waiting for transfers between devices, summed_over_col(): lax.psum_scatter(term_fn(jnp.int32(0), row_count * lax.axis_size('col')),...  225 us
    all_gather x4, waiting for transfers between devices, row_rows(): return lax.all_gather(values, 'row', axis=0, tiled=True)  195 us
    all_gather x4, waiting for transfers between devices, column_rows(): return lax.all_gather(values, 'col', axis=0, tiled=True)  127 us
    psum x4, blocking collectives, feature_totals(): return lax.psum(values, 'row')  41.7 us
    psum x1, blocking collectives, on_device(): lax.psum((ln1_gain_part, ln1_bias_part, qv_part, out_bias_part, ln2_gain_...  41.7 us
  transfers between devices with their start and end apart: 17, of which 17 were waited for; matrix products, arithmetic and copies ran while one was open for 7% of the time, Pallas kernels for 0%

commit v1 on v0

--- a/solution.py
+++ b/solution.py
@@ -11,6 +11,22 @@
 masked_score = -1e30
 
 
+def ring_gather(x, axis, dim):
+    ways, here, step = (lax.axis_size(axis), lax.axis_index(axis), x.shape[dim])
+    dims = [n * ways if d == dim else n for d, n in enumerate(x.shape)]
+    full = lax.dynamic_update_slice_in_dim(jnp.zeros(dims, x.dtype), x, here * step, axis=dim)
+    going_up = going_down = x
+    for far in range(1, ways // 2 + 1):
+        going_up = lax.ppermute(going_up, axis, [(d, (d + 1) % ways) for d in range(ways)])
+        full = lax.dynamic_update_slice_in_dim(full, going_up, (here - far) % ways * step, axis=dim)
+        if 2 * far < ways:
+            going_down = lax.ppermute(going_down, axis, [(d, (d - 1) % ways) for d in range(ways)])
+            full = lax.dynamic_update_slice_in_dim(
+                full, going_down, (here + far) % ways * step, axis=dim
+            )
+    return full
+
+
 def feature_totals(values):
     return lax.psum(values, "row")
 
@@ -20,7 +36,7 @@
 
 
 def row_rows(values):
-    return lax.all_gather(values, "row", axis=0, tiled=True)
+    return ring_gather(values, "row", 0)
 
 
 def summed_over_row(term_fn, row_count):

time: 1170 us -> 1240 us (1.060)
  waiting for transfers between devices: 924 us -> 968 us
  local copies, waits for them, and re-layouts: 18.6 us -> 35.9 us
  starting transfers between devices: 1.36 us -> 14 us
    ppermute x0 -> x12, waiting for transfers between devices: none -> 282 us  [the longest x8 221 us: ring_gather(): lax.ppermute(going_up, axis, [(d, (d + 1) % ways) for d in range(ways)])]
    all_gather x4 -> x0, waiting for transfers between devices: 195 us -> none  [row_rows(): return lax.all_gather(values, 'row', axis=0, tiled=True)]
    reduce_scatter x4, waiting for transfers between devices: 372 us -> 330 us  [summed_over_row(): lax.psum_scatter(term_fn(jnp.int32(0), row_count * lax.axis_size('row')),...]
    ppermute x0 -> x12, starting transfers between devices: none -> 13 us  [the longest x8 7.09 us: ring_gather(): lax.ppermute(going_up, axis, [(d, (d + 1) % ways) for d in range(ways)])]
  transfers between devices with their start and end apart: 17 -> 25, of which waited for: 17 -> 25; matrix products, arithmetic and copies ran while one was open for 7% -> 7% of each run, Pallas kernels for 0% -> 0%
where the time goes in v1:
time: 1240 us; the launch traced here: 1230 us
  waiting for transfers between devices  968 us (78%)
  blocking collectives  83.3 us (7%)
  matrix products  74.4 us (6%)
  other arithmetic  39.4 us (3%)
  local copies, waits for them, and re-layouts  35.9 us (3%)
  between operations  15.6 us (1%)
  starting transfers between devices  14 us (1%)
    reduce_scatter x4, waiting for transfers between devices, summed_over_row(): lax.psum_scatter(term_fn(jnp.int32(0), row_count * lax.axis_size('row')),...  330 us
    reduce_scatter x4, waiting for transfers between devices, summed_over_col(): lax.psum_scatter(term_fn(jnp.int32(0), row_count * lax.axis_size('col')),...  225 us
    ppermute x8, waiting for transfers between devices, ring_gather(): lax.ppermute(going_up, axis, [(d, (d + 1) % ways) for d in range(ways)])  221 us
    all_gather x4, waiting for transfers between devices, column_rows(): return lax.all_gather(values, 'col', axis=0, tiled=True)  126 us
    ppermute x4, waiting for transfers between devices, ring_gather(): lax.ppermute(going_down, axis, [(d, (d - 1) % ways) for d in range(ways)])  61.3 us
    psum x1, blocking collectives, on_device(): lax.psum((ln1_gain_part, ln1_bias_part, qv_part, out_bias_part, ln2_gain_...  41.6 us
    psum x4, blocking collectives, feature_totals(): return lax.psum(values, 'row')  41.6 us
  transfers between devices with their start and end apart: 25, of which 25 were waited for; matrix products, arithmetic and copies ran while one was open for 7% of the time, Pallas kernels for 0%

profile of v1, /device:TPU:0, one launch (start us, length us, event | category | flops | bytes accessed | tf_op | source)
XLA Modules:
  0.0 1230.8 jit_solution(15873586180413765703)
XLA Ops:
  11.0 11.5 all-reduce.4
  22.5 1.9 fusion.38
  25.7 35.4 %all-gather.5.cloned.1.call-done = bf16[4096,192]{0,1:T(8,128)(2,1)} async-done(((bf16[1024,192]{0,1:T(8,128)(2,1)}), bf16[4096,192]{0,1:T(8,128)(2,1)}) %all-gather.5.cloned.1.call-update) | async-done | bytes 1572880 | tf_op jit(solution)/shard_map/all_gather | solution.py:35
  61.1 6.4 fusion.61
  69.6 92.0 %reduce-scatter.9.cloned.1.call-done = f32[1024,3,192]{0,2,1:T(8,128)} async-done(((f32[4096,3,192]{0,2,1:T(8,128)}), f32[1024,3,192]{0,2,1:T(8,128)}) %reduce-scatter.9.cloned.1.call-update) | async-done | bytes 2359312 | tf_op jit(solution)/shard_map/reduce_scatter | solution.py:43
  161.6 1.9 add_convert_fusion
  163.5 3.2 fusion.55
  168.6 2.8 copy-done.2
  171.4 2.3 fusion.21
  176.7 10.0 collective-permute-done
  187.4 7.6 collective-permute-done.1
  195.0 7.3 collective-permute-done.2
  202.4 2.2 fusion.56
  207.6 57.4 %reduce-scatter.11.cloned.1.call-done = f32[1024,192]{0,1:T(8,128)} async-done(((f32[4096,192]{0,1:T(8,128)}), f32[1024,192]{0,1:T(8,128)}) %reduce-scatter.11.cloned.1.call-update) | async-done | bytes 786448 | tf_op jit(solution)/shard_map/reduce_scatter | solution.py:52
  266.3 10.0 all-reduce.3
  277.5 26.1 %all-gather.9.cloned.1.call-done = bf16[4096,192]{0,1:T(8,128)(2,1)} async-done(((bf16[1024,192]{0,1:T(8,128)(2,1)}), bf16[4096,192]{0,1:T(8,128)(2,1)}) %all-gather.9.cloned.1.call-update) | async-done | bytes 1572880 | tf_op jit(solution)/shard_map/all_gather | solution.py:35
  303.6 7.8 fusion.59
  311.9 29.6 %all-gather.7.cloned.1.call-done = bf16[4096,192]{0,1:T(8,128)(2,1)} async-done(((bf16[1024,192]{0,1:T(8,128)(2,1)}), bf16[4096,192]{0,1:T(8,128)(2,1)}) %all-gather.7.cloned.1.call-update) | async-done | bytes 1572880 | tf_op jit(solution)/shard_map/all_gather | solution.py:35
  341.6 7.9 fusion.57
  350.3 113.8 %reduce-scatter.17.cloned.1.call-done = f32[1024,768]{1,0:T(8,128)} async-done(((f32[4096,768]{1,0:T(8,128)}), f32[1024,768]{1,0:T(8,128)}) %reduce-scatter.17.cloned.1.call-update) | async-done | bytes 3145744 | tf_op jit(solution)/shard_map/reduce_scatter | solution.py:43
  464.1 123.9 %reduce-scatter.13.cloned.1.call-done = f32[1024,768]{1,0:T(8,128)} async-done(((f32[4096,768]{1,0:T(8,128)}), f32[1024,768]{1,0:T(8,128)}) %reduce-scatter.13.cloned.1.call-update) | async-done | bytes 3145744 | tf_op jit(solution)/shard_map/reduce_scatter | solution.py:43
  588.0 4.9 convert_reduce_fusion
  595.8 35.3 %collective-permute-done.6 = bf16[1024,768]{1,0:T(8,128)(2,1)S(1)} collective-permute-done((bf16[1024,768]{1,0:T(8,128)(2,1)S(1)}, bf16[1024,768]{1,0:T(8,128)(2,1)S(1)}, u32[]{:S(2)}, u32[]{:S(2)}) %collective-permute-start.6) | collective-permute-done | bytes 1572896 | tf_op jit(solution)/shard_map/ppermute | solution.py:20
  632.2 32.4 %collective-permute-done.7 = bf16[1024,768]{1,0:T(8,128)(2,1)S(1)} collective-permute-done((bf16[1024,768]{1,0:T(8,128)(2,1)S(1)}, bf16[1024,768]{1,0:T(8,128)(2,1)S(1)}, u32[]{:S(2)}, u32[]{:S(2)}) %collective-permute-start.7) | collective-permute-done | bytes 1572896 | tf_op jit(solution)/shard_map/ppermute | solution.py:23
  664.8 32.5 %collective-permute-done.8 = bf16[1024,768]{1,0:T(8,128)(2,1)S(1)} collective-permute-done((bf16[1024,768]{1,0:T(8,128)(2,1)S(1)}, bf16[1024,768]{1,0:T(8,128)(2,1)S(1)}, u32[]{:S(2)}, u32[]{:S(2)}) %collective-permute-start.8) | collective-permute-done | bytes 1572896 | tf_op jit(solution)/shard_map/ppermute | solution.py:20
  697.5 2.6 copy-done.3
  700.1 3.9 fusion.60
  704.1 60.2 %reduce-scatter.19.cloned.1.call-done = f32[1024,192]{0,1:T(8,128)} async-done(((f32[4096,192]{0,1:T(8,128)}), f32[1024,192]{0,1:T(8,128)}) %reduce-scatter.19.cloned.1.call-update) | async-done | bytes 786448 | tf_op jit(solution)/shard_map/reduce_scatter | solution.py:52
  764.3 2.1 multiply_reduce_fusion.1
  766.4 10.0 all-reduce.2
  776.5 2.8 convert_reduce_fusion.4
  779.4 35.3 %all-gather.11.cloned.1.call-done = bf16[4096,192]{0,1:T(8,128)(2,1)} async-done(((bf16[1024,192]{0,1:T(8,128)(2,1)}), bf16[4096,192]{0,1:T(8,128)(2,1)}) %all-gather.11.cloned.1.call-update) | async-done | bytes 1572880 | tf_op jit(solution)/shard_map/all_gather | solution.py:35
  814.7 3.6 fusion.62
  818.4 3.1 broadcast.97.clone.1
  821.6 2.8 constant_dynamic-update-slice_fusion.11
  827.3 59.1 %collective-permute-done.3 = bf16[1024,768]{1,0:T(8,128)(2,1)} collective-permute-done((bf16[1024,768]{1,0:T(8,128)(2,1)}, bf16[1024,768]{1,0:T(8,128)(2,1)}, u32[]{:S(2)}, u32[]{:S(2)}) %collective-permute-start.3) | collective-permute-done | bytes 1572896 | tf_op jit(solution)/shard_map/ppermute | solution.py:20
  888.1 6.2 multiply_reduce_fusion
  896.5 5.3 multiply_convert_fusion
  901.8 4.1 fusion.16
  905.9 2.1 fusion.18
  908.1 2.0 fusion.17
  912.0 2.9 constant_dynamic-update-slice_fusion.10
  914.9 4.3 collective-permute-done.4
  919.1 2.7 constant_dynamic-update-slice_fusion.9
  921.8 2.2 convolution_convert_fusion.1
  925.2 28.7 %collective-permute-done.5 = bf16[1024,768]{1,0:T(8,128)(2,1)} collective-permute-done((bf16[1024,768]{1,0:T(8,128)(2,1)}, bf16[1024,768]{1,0:T(8,128)(2,1)}, u32[]{:S(2)}, u32[]{:S(2)}) %collective-permute-start.5) | collective-permute-done | bytes 1572896 | tf_op jit(solution)/shard_map/ppermute | solution.py:20
  953.8 2.7 constant_dynamic-update-slice_fusion.8
  956.5 22.5 %collective-permute-done.9 = bf16[1024,3,192]{0,2,1:T(8,128)(2,1)S(1)} collective-permute-done((bf16[1024,3,192]{0,2,1:T(8,128)(2,1)S(1)}, bf16[1024,3,192]{0,2,1:T(8,128)(2,1)S(1)}, u32[]{:S(2)}, u32[]{:S(2)}) %collective-permute-start.9) | collective-permute-done | bytes 1179680 | tf_op jit(solution)/shard_map/ppermute | solution.py:20
  979.2 4.9 fusion.25
  986.3 17.0 %collective-permute-done.10 = bf16[1024,3,192]{0,2,1:T(8,128)(2,1)S(1)} collective-permute-done((bf16[1024,3,192]{0,2,1:T(8,128)(2,1)S(1)}, bf16[1024,3,192]{0,2,1:T(8,128)(2,1)S(1)}, u32[]{:S(2)}, u32[]{:S(2)}) %collective-permute-start.10) | collective-permute-done | bytes 1179680 | tf_op jit(solution)/shard_map/ppermute | solution.py:23
  1003.4 25.6 %collective-permute-done.11 = bf16[1024,3,192]{0,2,1:T(8,128)(2,1)S(1)} collective-permute-done((bf16[1024,3,192]{0,2,1:T(8,128)(2,1)S(1)}, bf16[1024,3,192]{0,2,1:T(8,128)(2,1)S(1)}, u32[]{:S(2)}, u32[]{:S(2)}) %collective-permute-start.11) | collective-permute-done | bytes 1179680 | tf_op jit(solution)/shard_map/ppermute | solution.py:20
  1029.2 2.1 copy-done.4
  1031.3 2.1 fusion.26
  1033.5 5.4 convolution_bitcast_fusion
  1039.9 6.7 fusion.58
  1048.8 3.5 all-reduce.8.cloned.1.call-done
  1052.3 1.8 convert_element_type.121
  1054.1 1.8 convert_element_type.125
  1055.9 1.9 copy.34
  1059.5 56.6 %reduce-scatter.23.cloned.1.call-done = f32[1024,192]{0,1:T(8,128)} async-done(((f32[4096,192]{0,1:T(8,128)}), f32[1024,192]{0,1:T(8,128)}) %reduce-scatter.23.cloned.1.call-update) | async-done | bytes 786448 | tf_op jit(solution)/shard_map/reduce_scatter | solution.py:52
  1117.6 10.1 all-reduce.1
  1127.7 51.2 %reduce-scatter.15.cloned.1.call-done = f32[1024,192]{0,1:T(8,128)} async-done(((f32[4096,192]{0,1:T(8,128)}), f32[1024,192]{0,1:T(8,128)}) %reduce-scatter.15.cloned.1.call-update) | async-done | bytes 786448 | tf_op jit(solution)/shard_map/reduce_scatter | solution.py:52
  1178.9 2.9 fusion.43
  1182.4 41.6 %all-reduce = (f32[768]{0:T(1024)}, f32[768]{0:T(1024)}, f32[2,768]{1,0:T(2,128)}, f32[768]{0:T(1024)}, f32[768]{0:T(1024)}, /*index=5*/f32[768]{0:T(1024)}, f32[3072]{0:T(1024)}, f32[768]{0:T(1024)}) all-reduce(f32[768]{0:T(1024)S(1)} %dynamic_update_slice.97, ...), channel_id=1, replica_groups=mesh['dp'=2,'row'=4,'col'=4] {'dp','row','col'}, use_global_device_ids=true, to_apply=%region_28.29 | all-reduce | flops 9216 | bytes 73728 | tf_op jit(solution)/shard_map/psum | solution.py:280
  (216 shorter events, 42.5 us)
Async XLA Ops:
  7.2 334.4 %copy-start = (bf16[192,768]{1,0:T(8,128)(2,1)S(1)}, bf16[192,768]{1,0:T(8,128)(2,1)}, u32[]{:S(2)}) copy-start(bf16[192,768]{1,0:T(8,128)(2,1)} %param.25) | copy-start | bytes 884740
  7.2 53.9 %all-gather.5.cloned.1.call-start = ((), (), s32[]{:S(2)}) async-start(), calls=%async_computation.8 | async-start | bytes 1966080 | tf_op jit(solution)/shard_map/all_gather | solution.py:35
  10.2 14.3 %copy-start.45 = (f32[192]{0:T(256)}, f32[192]{0:T(256)S(1)}, u32[]{:S(2)}) copy-start(f32[192]{0:T(256)S(1)} %dynamic_slice.40) | copy-start | bytes 2308
  24.5 137.1 %reduce-scatter.9.cloned.1.call-start = ((), (), s32[]{:S(2)}) async-start(), calls=%async_computation.9 | async-start | bytes 11796480 | tf_op jit(solution)/shard_map/reduce_scatter | solution.py:43
  67.6 197.4 %reduce-scatter.11.cloned.1.call-start = ((), (), s32[]{:S(2)}) async-start(), calls=%async_computation.10 | async-start | bytes 3932160 | tf_op jit(solution)/shard_map/reduce_scatter | solution.py:52
  163.5 5.1 copy-start.16
  168.6 5.1 copy-start.29
  173.7 28.7 %copy-start.22 = (bf16[192,192]{1,0:T(8,128)(2,1)S(1)}, bf16[192,192]{1,0:T(8,128)(2,1)}, u32[]{:S(2)}) copy-start(bf16[192,192]{1,0:T(8,128)(2,1)} %param.21) | copy-start | bytes 221188
  173.7 13.0 %collective-permute-start = (bf16[1024,192]{0,1:T(8,128)(2,1)S(1)}, bf16[1024,192]{0,1:T(8,128)(2,1)S(1)}, u32[]{:S(2)}, u32[]{:S(2)}) collective-permute-start(bf16[1024,192]{0,1:T(8,128)(2,1)S(1)} %bitcast.140), channel_id=1, source_target_pairs={{0,4},{4,8},{8,12},{12,0},{1,5},{5,9},{9,13},{13,1},{2,6},{6,10},{... | collective-permute-start | bytes 1179656 | tf_op jit(solution)/shard_map/ppermute | solution.py:20
  175.1 19.9 %collective-permute-start.1 = (bf16[1024,192]{0,1:T(8,128)(2,1)S(1)}, bf16[1024,192]{0,1:T(8,128)(2,1)S(1)}, u32[]{:S(2)}, u32[]{:S(2)}) collective-permute-start(bf16[1024,192]{0,1:T(8,128)(2,1)S(1)} %bitcast.141), channel_id=1, source_target_pairs={{0,12},{4,0},{8,4},{12,8},{1,13},{5,1},{9,5},{13,9},{2,14},{6,2},{... | collective-permute-start | bytes 1179656 | tf_op jit(solution)/shard_map/ppermute | solution.py:23
  186.7 15.7 %collective-permute-start.2 = (bf16[1024,192]{0,1:T(8,128)(2,1)S(1)}, bf16[1024,192]{0,1:T(8,128)(2,1)S(1)}, u32[]{:S(2)}, u32[]{:S(2)}) collective-permute-start(bf16[1024,192]{0,1:T(8,128)(2,1)S(1)} %collective-permute-done), channel_id=1, source_target_pairs={{0,4},{4,8},{8,12},{12,0},{1,5},{5,9},{9,13},{13,1},{2,6},{6,10},{... | collective-permute-start | bytes 1179656 | tf_op jit(solution)/shard_map/ppermute | solution.py:20
  204.7 60.4 %copy-start.5 = (bf16[192,1024]{1,0:T(8,128)(2,1)S(1)}, bf16[192,1024]{1,0:T(8,128)(2,1)}, u32[]{:S(2)}) copy-start(bf16[192,1024]{1,0:T(8,128)(2,1)} %param.15) | copy-start | bytes 1179652
  204.7 98.9 %copy-start.20 = (bf16[192,768]{1,0:T(8,128)(2,1)S(1)}, bf16[192,768]{1,0:T(8,128)(2,1)}, u32[]{:S(2)}) copy-start(bf16[192,768]{1,0:T(8,128)(2,1)} %param.27) | copy-start | bytes 884740
  204.7 98.9 %all-gather.9.cloned.1.call-start = ((), (), s32[]{:S(2)}) async-start(), calls=%async_computation.14 | async-start | bytes 1966080 | tf_op jit(solution)/shard_map/all_gather | solution.py:35
  205.3 136.3 %all-gather.7.cloned.1.call-start = ((), (), s32[]{:S(2)}) async-start(), calls=%async_computation.11 | async-start | bytes 1966080 | tf_op jit(solution)/shard_map/all_gather | solution.py:35
  206.8 104.6 %copy-start.41 = (f32[192]{0:T(256)}, f32[192]{0:T(256)S(1)}, u32[]{:S(2)}) copy-start(f32[192]{0:T(256)S(1)} %dynamic_slice.44) | copy-start | bytes 2308
  276.4 35.0 %copy-start.23 = (f32[1024]{0:T(1024)}, f32[1024]{0:T(1024)S(1)}, u32[]{:S(2)}) copy-start(f32[1024]{0:T(1024)S(1)} %get-tuple-element.110) | copy-start | bytes 12292
  276.4 35.0 %copy-start.26 = (f32[1024]{0:T(1024)}, f32[1024]{0:T(1024)S(1)}, u32[]{:S(2)}) copy-start(f32[1024]{0:T(1024)S(1)} %get-tuple-element.111) | copy-start | bytes 12292
  277.4 186.7 %reduce-scatter.17.cloned.1.call-start = ((), (), s32[]{:S(2)}) async-start(), calls=%async_computation.15 | async-start | bytes 15728640 | tf_op jit(solution)/shard_map/reduce_scatter | solution.py:43
  311.4 276.6 %reduce-scatter.13.cloned.1.call-start = ((), (), s32[]{:S(2)}) async-start(), calls=%async_computation.12 | async-start | bytes 15728640 | tf_op jit(solution)/shard_map/reduce_scatter | solution.py:43
  349.4 414.9 %reduce-scatter.19.cloned.1.call-start = ((), (), s32[]{:S(2)}) async-start(), calls=%async_computation.16 | async-start | bytes 3932160 | tf_op jit(solution)/shard_map/reduce_scatter | solution.py:52
  350.3 242.6 %copy-start.35 = (f32[768]{0:T(1024)}, f32[768]{0:T(1024)S(1)}, u32[]{:S(2)}) copy-start(f32[768]{0:T(1024)S(1)} %dynamic_slice.46) | copy-start | bytes 9220
  592.9 38.2 %collective-permute-start.6 = (bf16[1024,768]{1,0:T(8,128)(2,1)S(1)}, bf16[1024,768]{1,0:T(8,128)(2,1)S(1)}, u32[]{:S(2)}, u32[]{:S(2)}) collective-permute-start(bf16[1024,768]{1,0:T(8,128)(2,1)S(1)} %get-tuple-element.92), channel_id=1, source_target_pairs={{0,4},{4,8},{8,12},{12,0},{1,5},{5,9},{9,13},{13,1},{2,6},{6,10},{... | collective-permute-start | bytes 4718600 | tf_op jit(solution)/shard_map/ppermute | solution.py:20
  594.2 70.5 %collective-permute-start.7 = (bf16[1024,768]{1,0:T(8,128)(2,1)S(1)}, bf16[1024,768]{1,0:T(8,128)(2,1)S(1)}, u32[]{:S(2)}, u32[]{:S(2)}) collective-permute-start(bf16[1024,768]{1,0:T(8,128)(2,1)S(1)} %get-tuple-element.92), channel_id=1, source_target_pairs={{0,12},{4,0},{8,4},{12,8},{1,13},{5,1},{9,5},{13,9},{2,14},{6,2},{... | collective-permute-start | bytes 4718600 | tf_op jit(solution)/shard_map/ppermute | solution.py:23
  631.0 66.3 %collective-permute-start.8 = (bf16[1024,768]{1,0:T(8,128)(2,1)S(1)}, bf16[1024,768]{1,0:T(8,128)(2,1)S(1)}, u32[]{:S(2)}, u32[]{:S(2)}) collective-permute-start(bf16[1024,768]{1,0:T(8,128)(2,1)S(1)} %collective-permute-done.6), channel_id=1, source_target_pairs={{0,4},{4,8},{8,12},{12,0},{1,5},{5,9},{9,13},{13,1},{2,6},{6,10},{... | collective-permute-start | bytes 4718600 | tf_op jit(solution)/shard_map/ppermute | solution.py:20
  704.0 60.3 %copy-start.24 = (f32[1024]{0:T(1024)S(1)}, f32[1024]{0:T(1024)}, u32[]{:S(2)}) copy-start(f32[1024]{0:T(1024)} %copy-done.23) | copy-start | bytes 12292
  704.0 60.3 %copy-start.27 = (f32[1024]{0:T(1024)S(1)}, f32[1024]{0:T(1024)}, u32[]{:S(2)}) copy-start(f32[1024]{0:T(1024)} %copy-done.26) | copy-start | bytes 12292
  704.0 60.3 %copy-start.42 = (f32[192]{0:T(256)S(1)}, f32[192]{0:T(256)}, u32[]{:S(2)}) copy-start(f32[192]{0:T(256)} %copy-done.41) | copy-start | bytes 2308
  704.0 72.5 %copy-start.8 = (bf16[192,1024]{1,0:T(8,128)(2,1)S(1)}, bf16[192,1024]{1,0:T(8,128)(2,1)}, u32[]{:S(2)}) copy-start(bf16[192,1024]{1,0:T(8,128)(2,1)} %param.29) | copy-start | bytes 1179652
  704.0 110.7 %all-gather.11.cloned.1.call-start = ((), (), s32[]{:S(2)}) async-start(), calls=%async_computation.17 | async-start | bytes 1966080 | tf_op jit(solution)/shard_map/all_gather | solution.py:35
  776.5 41.9 %copy-start.37 = (f32[1024]{0:T(1024)}, f32[1024]{0:T(1024)S(1)}, u32[]{:S(2)}) copy-start(f32[1024]{0:T(1024)S(1)} %get-tuple-element.118) | copy-start | bytes 12292
  776.5 41.8 %copy-start.39 = (f32[1024]{0:T(1024)}, f32[1024]{0:T(1024)S(1)}, u32[]{:S(2)}) copy-start(f32[1024]{0:T(1024)S(1)} %get-tuple-element.119) | copy-start | bytes 12292
  779.3 107.6 %reduce-scatter.21.cloned.1.call-start = ((), (), s32[]{:S(2)}) async-start(), calls=%async_computation.18 | async-start | bytes 3932160 | tf_op jit(solution)/shard_map/reduce_scatter | solution.py:43
  818.4 233.9 %all-reduce.8.cloned.1.call-start = ((), (), s32[]{:S(2)}) async-start(), calls=%async_computation.20 | async-start | bytes 1966080 | tf_op jit(solution)/shard_map/psum | solution.py:294
  824.4 62.1 %collective-permute-start.3 = (bf16[1024,768]{1,0:T(8,128)(2,1)}, bf16[1024,768]{1,0:T(8,128)(2,1)}, u32[]{:S(2)}, u32[]{:S(2)}) collective-permute-start(bf16[1024,768]{1,0:T(8,128)(2,1)} %get-tuple-element.98), channel_id=1, source_target_pairs={{0,4},{4,8},{8,12},{12,0},{1,5},{5,9},{9,13},{13,1},{2,6},{6,10},{... | collective-permute-start | bytes 4718600 | tf_op jit(solution)/shard_map/ppermute | solution.py:20
  825.9 93.3 %collective-permute-start.4 = (bf16[1024,768]{1,0:T(8,128)(2,1)}, bf16[1024,768]{1,0:T(8,128)(2,1)}, u32[]{:S(2)}, u32[]{:S(2)}) collective-permute-start(bf16[1024,768]{1,0:T(8,128)(2,1)} %get-tuple-element.98), channel_id=1, source_target_pairs={{0,12},{4,0},{8,4},{12,8},{1,13},{5,1},{9,5},{13,9},{2,14},{6,2},{... | collective-permute-start | bytes 4718600 | tf_op jit(solution)/shard_map/ppermute | solution.py:23
  886.4 67.4 %collective-permute-start.5 = (bf16[1024,768]{1,0:T(8,128)(2,1)}, bf16[1024,768]{1,0:T(8,128)(2,1)}, u32[]{:S(2)}, u32[]{:S(2)}) collective-permute-start(bf16[1024,768]{1,0:T(8,128)(2,1)} %collective-permute-done.3), channel_id=1, source_target_pairs={{0,4},{4,8},{8,12},{12,0},{1,5},{5,9},{9,13},{13,1},{2,6},{6,10},{... | collective-permute-start | bytes 4718600 | tf_op jit(solution)/shard_map/ppermute | solution.py:20
  888.1 6.3 slice-start
  888.1 7.2 slice-start.1
  888.1 8.4 slice-start.2
  896.5 5.3 copy-start.13
  901.8 6.2 slice-start.3
  908.0 13.8 %slice-start.5 = ((s8[6291456]{0:T(1024)(128)(4,1)}), s8[2097152]{0:T(1024)(128)(4,1)S(1)}, s32[]{:S(2)}) async-start(s8[6291456]{0:T(1024)(128)(4,1)} %bitcast.125), calls=%async_computation.26 | async-start | bytes 4194304
  910.1 11.7 slice-start.6
  910.3 68.7 %collective-permute-start.9 = (bf16[1024,3,192]{0,2,1:T(8,128)(2,1)S(1)}, bf16[1024,3,192]{0,2,1:T(8,128)(2,1)S(1)}, u32[]{:S(2)}, u32[]{:S(2)}) collective-permute-start(bf16[1024,3,192]{0,2,1:T(8,128)(2,1)S(1)} %get-tuple-element.96), channel_id=1, source_target_pairs={{0,4},{4,8},{8,12},{12,0},{1,5},{5,9},{9,13},{13,1},{2,6},{6,10},{... | collective-permute-start | bytes 3538952 | tf_op jit(solution)/shard_map/ppermute | solution.py:20
  912.0 9.8 copy-start.15
  924.0 55.2 %copy-start.14 = (bf16[4096,192]{0,1:T(8,128)(2,1)S(1)}, bf16[4096,192]{0,1:T(8,128)(2,1)}, u32[]{:S(2)}) copy-start(bf16[4096,192]{0,1:T(8,128)(2,1)} %all-gather.9.cloned.1.call-done) | copy-start | bytes 4718596
  924.0 79.3 %collective-permute-start.10 = (bf16[1024,3,192]{0,2,1:T(8,128)(2,1)S(1)}, bf16[1024,3,192]{0,2,1:T(8,128)(2,1)S(1)}, u32[]{:S(2)}, u32[]{:S(2)}) collective-permute-start(bf16[1024,3,192]{0,2,1:T(8,128)(2,1)S(1)} %get-tuple-element.96), channel_id=1, source_target_pairs={{0,12},{4,0},{8,4},{12,8},{1,13},{5,1},{9,5},{13,9},{2,14},{6,2},{... | collective-permute-start | bytes 3538952 | tf_op jit(solution)/shard_map/ppermute | solution.py:23
  956.5 27.6 %copy-start.18 = (bf16[4096,192]{0,1:T(8,128)(2,1)S(1)}, bf16[4096,192]{0,1:T(8,128)(2,1)}, u32[]{:S(2)}) copy-start(bf16[4096,192]{0,1:T(8,128)(2,1)} %all-gather.11.cloned.1.call-done) | copy-start | bytes 4718596
  979.0 50.0 %collective-permute-start.11 = (bf16[1024,3,192]{0,2,1:T(8,128)(2,1)S(1)}, bf16[1024,3,192]{0,2,1:T(8,128)(2,1)S(1)}, u32[]{:S(2)}, u32[]{:S(2)}) collective-permute-start(bf16[1024,3,192]{0,2,1:T(8,128)(2,1)S(1)} %collective-permute-done.9), channel_id=1, source_target_pairs={{0,4},{4,8},{8,12},{12,0},{1,5},{5,9},{9,13},{13,1},{2,6},{6,10},{... | collective-permute-start | bytes 3538952 | tf_op jit(solution)/shard_map/ppermute | solution.py:20
  986.1 45.2 %copy-start.17 = (bf16[4096,192]{0,1:T(8,128)(2,1)S(1)}, bf16[4096,192]{0,1:T(8,128)(2,1)}, u32[]{:S(2)}) copy-start(bf16[4096,192]{0,1:T(8,128)(2,1)} %all-gather.5.cloned.1.call-done) | copy-start | bytes 4718596
  1033.5 82.6 %reduce-scatter.23.cloned.1.call-start = ((), (), s32[]{:S(2)}) async-start(), calls=%async_computation.19 | async-start | bytes 3932160 | tf_op jit(solution)/shard_map/reduce_scatter | solution.py:52
  1039.0 139.8 %reduce-scatter.15.cloned.1.call-start = ((), (), s32[]{:S(2)}) async-start(), calls=%async_computation.13 | async-start | bytes 3932160 | tf_op jit(solution)/shard_map/reduce_scatter | solution.py:52
  1046.7 69.4 %copy-start.32 = (f32[1024]{0:T(1024)S(1)}, f32[1024]{0:T(1024)}, u32[]{:S(2)}) copy-start(f32[1024]{0:T(1024)} %copy-done.31) | copy-start | bytes 12292
  1046.7 69.4 %copy-start.34 = (f32[1024]{0:T(1024)S(1)}, f32[1024]{0:T(1024)}, u32[]{:S(2)}) copy-start(f32[1024]{0:T(1024)} %copy-done.33) | copy-start | bytes 12292
  1046.7 69.4 %copy-start.46 = (f32[192]{0:T(256)S(1)}, f32[192]{0:T(256)}, u32[]{:S(2)}) copy-start(f32[192]{0:T(256)} %copy-done.45) | copy-start | bytes 2308
  1046.7 132.1 %copy-start.7 = (f32[1024,192]{0,1:T(8,128)S(1)}, f32[1024,192]{0,1:T(8,128)}, u32[]{:S(2)}) copy-start(f32[1024,192]{0,1:T(8,128)} %reduce-scatter.19.cloned.1.call-done) | copy-start | bytes 2359300
  1046.7 132.1 %copy-start.9 = (bf16[192,1024]{1,0:T(8,128)(2,1)S(1)}, bf16[192,1024]{1,0:T(8,128)(2,1)}, u32[]{:S(2)}) copy-start(bf16[192,1024]{1,0:T(8,128)(2,1)} %param.29) | copy-start | bytes 1179652
  1046.7 132.1 %copy-start.25 = (f32[1024]{0:T(1024)S(1)}, f32[1024]{0:T(1024)}, u32[]{:S(2)}) copy-start(f32[1024]{0:T(1024)} %copy-done.23) | copy-start | bytes 12292
  1046.7 132.1 %copy-start.28 = (f32[1024]{0:T(1024)S(1)}, f32[1024]{0:T(1024)}, u32[]{:S(2)}) copy-start(f32[1024]{0:T(1024)} %copy-done.26) | copy-start | bytes 12292
  1046.7 132.1 %copy-start.38 = (f32[1024]{0:T(1024)S(1)}, f32[1024]{0:T(1024)}, u32[]{:S(2)}) copy-start(f32[1024]{0:T(1024)} %copy-done.37) | copy-start | bytes 12292
  1046.7 132.1 %copy-start.40 = (f32[1024]{0:T(1024)S(1)}, f32[1024]{0:T(1024)}, u32[]{:S(2)}) copy-start(f32[1024]{0:T(1024)} %copy-done.39) | copy-start | bytes 12292
  1046.8 132.1 %copy-start.43 = (f32[192]{0:T(256)S(1)}, f32[192]{0:T(256)}, u32[]{:S(2)}) copy-start(f32[192]{0:T(256)} %copy-done.41) | copy-start | bytes 2308
  1057.9 166.2 %copy-start.1 = (bf16[192,768]{1,0:T(8,128)(2,1)S(1)}, bf16[192,768]{1,0:T(8,128)(2,1)}, u32[]{:S(2)}) copy-start(bf16[192,768]{1,0:T(8,128)(2,1)} %param.25) | copy-start | bytes 884740
  (18 other events, 43.4 us)
Sparse Core Ops, SparseCore 0:
  24.6 36.4 all-gather.4
  67.7 93.8 reduce-scatter.8
  204.8 60.1 reduce-scatter.10
  266.4 37.1 all-gather.8
  305.6 35.9 all-gather.6
  344.5 119.5 reduce-scatter.16
  467.2 120.7 reduce-scatter.12
  704.2 60.1 reduce-scatter.18
  779.5 35.2 all-gather.10
  818.5 68.3 reduce-scatter.20
  1033.6 18.6 all-reduce.7
  1054.6 61.4 reduce-scatter.22
  1118.5 60.2 reduce-scatter.14
